TPU v7x, 256 devices: a whole 4x4x8 slice. The times are simulated.
256 devices in a mesh: col: 32 (over x_hi, z, core), row: 8 (over x_lo, y).
Axes of the slice: x: 4 (x_hi: 2, x_lo: 2; x = x_hi * 2 + x_lo), y: 4, z: 8, core: 2. Of those that a mesh axis runs over, the one named last changes fastest.
Arguments:
- matrix: float32 [64, 64, 128, 128], P('col', 'row'), may hold values from -12 to 80, as said below
- col_owner: int32 [64], replicated, may hold values from 0 to 63, as said below
- row_owner: int32 [64], replicated, may hold values from 0 to 63, as said below
- pattern: int32 [2, 64], replicated, may hold values from 0 to 1, as said below
Outputs:
- factored: float32 [64, 64, 128, 128], P('col', 'row')
Inputs may be any that keep to these rules, and one draw needn't show every extreme that they name: `col_owner`: a permutation of 0 to 63. `row_owner`: a permutation of 0 to 63. pattern[0, 1] is 1; pattern[k, i] is 0 for i <= k; pattern[1, i] >= pattern[0, i] for every i >= 2. `matrix`: the diagonal tile of every supernode is symmetric positive definite, and so is every diagonal tile after the updates.
All inputs are finite; a program needn't handle non-finite values.
Results may differ from a plain program's by a relative error of at most 0.0003.
Values sent between devices are 32-bit elements; how exact they have to be, the bound alone decides.
A program may use at most 64 MiB of HBM per device.

v0:
```python
import jax
import jax.numpy as jnp
from jax import lax
from jax.sharding import PartitionSpec as P

PRECISE = lax.Precision.HIGHEST


def broadcast(block, axis, source):
    block = jnp.where(lax.axis_index(axis) == source, block, jnp.zeros_like(block))
    return lax.psum(block, axis)


def owned_nodes(owner_map, first_place, how_many):
    places = first_place + jnp.arange(how_many, dtype=jnp.int32)
    ordinal = jnp.arange(owner_map.shape[0], dtype=jnp.int32)
    matches = owner_map[None, :] == places[:, None]
    return jnp.sum(jnp.where(matches, ordinal[None, :], 0), axis=1)


def diag_factor(diag_tile):
    lower_tri = jnp.linalg.cholesky(diag_tile)
    identity = jnp.eye(lower_tri.shape[0], dtype=lower_tri.dtype)
    return (lower_tri, lax.linalg.triangular_solve(lower_tri, identity, left_side=True, lower=True))


def solve_rows(tile_rows, inverse, kept_rows):
    scaled = jnp.einsum("spq,rq->spr", tile_rows, inverse, precision=PRECISE)
    return jnp.where(kept_rows[:, None, None], scaled, jnp.zeros_like(scaled))


def schur_apply(matrix, row_factors, col_factors, row_node, col_node):
    product = jnp.einsum("spq,lrq->lspr", row_factors, col_factors, precision=PRECISE)
    lower_half = row_node[None, :] >= col_node[:, None]
    return matrix - jnp.where(lower_half[:, :, None, None], product, jnp.zeros_like(product))


def write_back(matrix, local_col, is_owner, lower_tri, row_factors, kept_rows, row_node, panel_id):
    old_column = lax.dynamic_index_in_dim(matrix, local_col, 0, keepdims=False)
    is_diag = row_node == panel_id
    new_column = jnp.where(
        is_diag[:, None, None],
        lower_tri[None],
        jnp.where(kept_rows[:, None, None], row_factors, old_column),
    )
    new_column = jnp.where(is_owner, new_column, old_column)
    return lax.dynamic_update_index_in_dim(matrix, new_column, local_col, 0)


def body(matrix, col_owner, row_owner, pattern):
    cols_here = matrix.shape[0]
    slots_here = matrix.shape[1]
    col_rank = lax.axis_index("col")
    row_rank = lax.axis_index("row")
    first_slot = row_rank * slots_here
    col_node = owned_nodes(col_owner, col_rank * cols_here, cols_here)
    row_node = owned_nodes(row_owner, first_slot, slots_here)
    source_slot = row_owner[col_node]
    for panel_id in range(2):
        position = col_owner[panel_id]
        owner_col = position // cols_here
        local_col = position % cols_here
        diag_slot = row_owner[panel_id]
        kept_rows = pattern[panel_id][row_node] == 1
        kept_cols = pattern[panel_id][col_node] == 1
        raw_column = lax.dynamic_index_in_dim(matrix, local_col, 0, keepdims=False)
        gathered = lax.all_gather(raw_column, "row", axis=0, tiled=True)
        whole_column = broadcast(gathered, "col", owner_col)
        lower_tri, inverse = diag_factor(
            lax.dynamic_index_in_dim(whole_column, diag_slot, 0, keepdims=False)
        )
        my_rows = lax.dynamic_slice_in_dim(whole_column, first_slot, slots_here, 0)
        row_factors = solve_rows(my_rows, inverse, kept_rows)
        col_factors = solve_rows(jnp.take(whole_column, source_slot, axis=0), inverse, kept_cols)
        matrix = schur_apply(matrix, row_factors, col_factors, row_node, col_node)
        matrix = write_back(
            matrix,
            local_col,
            col_rank == owner_col,
            lower_tri,
            row_factors,
            kept_rows,
            row_node,
            panel_id,
        )
    return matrix


def solution(mesh):
    return jax.shard_map(
        body,
        mesh=mesh,
        in_specs=(P("col", "row", None, None), P(), P(), P()),
        out_specs=P("col", "row", None, None),
        check_vma=False,
    )
```

profile of v0, /device:TPU:1, one launch (start us, length us, event | category | flops | bytes accessed | tf_op | source)
XLA Modules:
  0.0 762.4 jit_solution(656796158354332296)
XLA Ops:
  6.5 1.3 fusion.38
  10.0 1.9 dynamic-slice_bitcast_fusion
  12.6 58.1 %all-gather.5.cloned.1.call-done = f32[1,64,128,128]{3,2,0,1:T(8,128)} async-done(((f32[1,8,128,128]{3,2,0,1:T(8,128)}), f32[1,64,128,128]{3,2,0,1:T(8,128)}) %all-gather.5.cloned.1.call-update) | async-done | bytes 4194320 | tf_op jit(solution)/shard_map/all_gather | solution.py:67
  70.7 4.7 fusion.1
  77.3 0.6 fusion.37
  79.2 0.3 copy.35
  79.5 0.2 fusion.31
  79.7 0.6 gather_fusion.1
  80.4 0.6 gather_fusion
  81.0 0.2 select_reduce_fusion.2
  81.2 0.6 gather_fusion.2
  82.7 271.2 %all-reduce.3.cloned.1.call-done = f32[64,128,128]{2,1,0:T(8,128)} async-done(((f32[64,128,128]{2,1,0:T(8,128)}), f32[64,128,128]{2,1,0:T(8,128)}) %all-reduce.3.cloned.1.call-update) | async-done | bytes 4194320 | tf_op jit(solution)/shard_map/psum | solution.py:11
  353.9 0.8 constant_dynamic-slice_fusion.4
  354.8 0.9 fusion.21
  355.7 11.7 %cholesky.44 = f32[128,128]{1,0:T(8,128)S(1)} custom-call(f32[128,128]{1,0:T(8,128)S(1)} %fusion.21), custom_call_target="Cholesky" | custom-call | tf_op jit(solution)/shard_map/jit(cholesky)/cholesky | solution.py:22
  367.4 0.6 compare_reduce_fusion.1
  368.1 0.7 select_bitcast_fusion.1
  368.7 9.8 %custom-call.6 = f32[1,128,128]{1,2,0:T(8,128)S(1)} custom-call(f32[1,128,128]{2,1,0:T(8,128)S(1)} %get-tuple-element.10), custom_call_target="InvertDiagBlocksLowerTriangular" | custom-call | tf_op jit(solution)/shard_map/triangular_solve/custom-call.0 | solution.py:24
  378.5 0.3 convolution_bitcast_fusion.1
  378.8 2.7 gather_fusion.5
  381.6 0.3 fusion.7
  381.9 1.6 convolution_select_fusion.3
  383.5 1.0 fusion.3
  384.6 0.2 copy.36
  384.8 0.2 fusion.12
  385.0 0.2 copy.37
  385.3 1.0 copy.38
  386.3 0.2 all-reduce.5.cloned.1.call-start
  387.2 52.9 %all-gather.7.cloned.1.call-done = f32[1,64,128,128]{3,2,0,1:T(8,128)} async-done(((f32[1,8,128,128]{3,2,0,1:T(8,128)}), f32[1,64,128,128]{3,2,0,1:T(8,128)}) %all-gather.7.cloned.1.call-update) | async-done | bytes 4194320 | tf_op jit(solution)/shard_map/all_gather | solution.py:67
  440.0 4.7 fusion
  445.9 0.6 gather_fusion.3
  446.6 0.6 gather_fusion.4
  447.9 275.3 %all-reduce.5.cloned.1.call-done = f32[64,128,128]{2,1,0:T(8,128)} async-done(((f32[64,128,128]{2,1,0:T(8,128)}), f32[64,128,128]{2,1,0:T(8,128)}) %all-reduce.5.cloned.1.call-update) | async-done | bytes 4194320 | tf_op jit(solution)/shard_map/psum | solution.py:11
  723.2 0.8 constant_dynamic-slice_fusion.1
  724.1 0.9 fusion.20
  725.0 11.7 %cholesky.55 = f32[128,128]{1,0:T(8,128)S(1)} custom-call(f32[128,128]{1,0:T(8,128)S(1)} %fusion.20), custom_call_target="Cholesky" | custom-call | tf_op jit(solution)/shard_map/jit(cholesky)/cholesky | solution.py:22
  736.7 0.6 compare_reduce_fusion
  737.3 0.7 select_bitcast_fusion
  738.0 9.8 %custom-call.7 = f32[1,128,128]{1,2,0:T(8,128)S(1)} custom-call(f32[1,128,128]{2,1,0:T(8,128)S(1)} %get-tuple-element.6), custom_call_target="InvertDiagBlocksLowerTriangular" | custom-call | tf_op jit(solution)/shard_map/triangular_solve/custom-call.0 | solution.py:24
  747.8 0.3 convolution_bitcast_fusion
  748.1 2.7 gather_fusion.6
  750.9 0.3 fusion.6
  751.2 1.6 convolution_select_fusion.2
  752.8 1.0 fusion.5
  753.9 0.2 copy.42
  754.1 0.2 fusion.9
  754.3 0.2 copy.43
  754.6 1.3 copy.44
  (38 shorter events, 0.8 us)
Async XLA Ops:
  6.5 64.2 %all-gather.5.cloned.1.call-start = ((), (), s32[]{:S(2)}) async-start(), calls=%async_computation.2 | async-start | bytes 4718592 | tf_op jit(solution)/shard_map/all_gather | solution.py:67
  11.9 342.0 %all-reduce.3.cloned.1.call-start = ((), (), s32[]{:S(2)}) async-start(), calls=%async_computation | async-start | bytes 8388608 | tf_op jit(solution)/shard_map/psum | solution.py:11
  75.4 1.9 copy-start
  75.4 3.8 copy-start.1
  75.4 4.2 copy-start.2
  75.4 5.0 copy-start.3
  75.4 364.6 %all-gather.7.cloned.1.call-start = ((), (), s32[]{:S(2)}) async-start(), calls=%async_computation.3 | async-start | bytes 4718592 | tf_op jit(solution)/shard_map/all_gather | solution.py:67
  386.3 336.8 %all-reduce.5.cloned.1.call-start = ((), (), s32[]{:S(2)}) async-start(), calls=%async_computation.1 | async-start | bytes 8388608 | tf_op jit(solution)/shard_map/psum | solution.py:11
Sparse Core Ops, SparseCore 0:
  12.0 58.6 all-gather.4
  75.5 278.2 all-reduce.2
  386.4 53.5 all-gather.6
  444.8 278.2 all-reduce.4
where the time goes:
time: 763 us; the launch traced here: 762 us
  waiting for transfers between devices  657 us (86%)
  other arithmetic  57.6 us (8%)
  between operations  22.5 us (3%)
  local copies, waits for them, and re-layouts  18 us (2%)
    psum x2, waiting for transfers between devices, broadcast(): return lax.psum(block, axis)  546 us
    all_gather x2, waiting for transfers between devices, body(): gathered = lax.all_gather(raw_column, 'row', axis=0, tiled=True)  111 us
    another operation x6, other arithmetic, diag_factor(): lower_tri = jnp.linalg.cholesky(diag_tile)  24.8 us
    another operation x4, other arithmetic, diag_factor(): lax.linalg.triangular_solve(lower_tri, identity, left_side=True, lower=True)  20.9 us
  transfers between devices with their start and end apart: 4, of which 4 were waited for; matrix products, arithmetic and copies ran while one was open for 1% of the time, Pallas kernels for 0%

commit v1 on v0

v1 whole, which is shorter than its diff:
```python
import jax
import jax.numpy as jnp
from jax import lax
from jax.sharding import PartitionSpec as P

PRECISE = lax.Precision.HIGHEST


def owned_nodes(owner_map, first_place, how_many):
    places = first_place + jnp.arange(how_many, dtype=jnp.int32)
    ordinal = jnp.arange(owner_map.shape[0], dtype=jnp.int32)
    matches = owner_map[None, :] == places[:, None]
    return jnp.sum(jnp.where(matches, ordinal[None, :], 0), axis=1)


def diag_factor(diag_tile):
    lower_tri = jnp.linalg.cholesky(diag_tile)
    identity = jnp.eye(lower_tri.shape[0], dtype=lower_tri.dtype)
    return (lower_tri, lax.linalg.triangular_solve(lower_tri, identity, left_side=True, lower=True))


def times_transposed(tiles, right):
    return jnp.einsum("...pq,rq->...pr", tiles, right, precision=PRECISE)


def keep_where(mask, tiles):
    return jnp.where(mask[..., None, None], tiles, jnp.zeros_like(tiles))


def body(matrix, col_owner, row_owner, pattern):
    cols_here = matrix.shape[0]
    slots_here = matrix.shape[1]
    col_rank = lax.axis_index("col")
    row_rank = lax.axis_index("row")
    first_slot = row_rank * slots_here
    col_node = owned_nodes(col_owner, col_rank * cols_here, cols_here)
    row_node = owned_nodes(row_owner, first_slot, slots_here)
    source_slot = row_owner[col_node]

    def own_tile(panel_id, slot):
        position = col_owner[panel_id]
        here = (position // cols_here == col_rank) & (slot // slots_here == row_rank)
        return keep_where(here, matrix[position % cols_here, slot % slots_here])

    leading = jnp.stack([own_tile(0, row_owner[0]), own_tile(0, row_owner[1]), own_tile(1, row_owner[1])])
    leading = lax.psum(leading, ("col", "row"))

    columns = jnp.stack(
        [
            keep_where(col_owner[k] // cols_here == col_rank, matrix[col_owner[k] % cols_here])
            for k in range(2)
        ]
    )
    columns, leading = lax.optimization_barrier((columns, leading))
    columns = lax.psum(columns, "col")

    held = source_slot // slots_here == row_rank
    across = keep_where(held[None, :], jnp.take(columns, source_slot % slots_here, axis=1))
    across = lax.psum(across, "row")

    lower_0, inverse_0 = diag_factor(leading[0])
    kept_next = jnp.where(pattern[0, 1] == 1, 1.0, 0.0).astype(jnp.float32)
    link = times_transposed(leading[1], inverse_0) * kept_next
    lower_1, inverse_1 = diag_factor(leading[2] - times_transposed(link, link))

    def factors(raw, nodes):
        kept = pattern[:, nodes] == 1
        first = keep_where(kept[0], times_transposed(raw[0], inverse_0))
        second = raw[1] - keep_where(nodes >= 1, times_transposed(first, link))
        second = keep_where(kept[1], times_transposed(second, inverse_1))
        return first, second

    row_factors = factors(columns, row_node)
    col_factors = factors(across, col_node)
    product = jnp.einsum(
        "spq,lrq->lspr",
        jnp.concatenate(row_factors, axis=-1),
        jnp.concatenate(col_factors, axis=-1),
        precision=PRECISE,
    )
    lower_half = row_node[None, :] >= col_node[:, None]
    matrix = matrix - keep_where(lower_half, product)

    for panel_id, lower_tri in enumerate((lower_0, lower_1)):
        mine = (col_node == panel_id)[:, None]
        is_diag = mine & (row_node == panel_id)[None, :]
        is_kept = mine & (pattern[panel_id][row_node] == 1)[None, :]
        matrix = jnp.where(is_kept[..., None, None], row_factors[panel_id][None], matrix)
        matrix = jnp.where(is_diag[..., None, None], lower_tri, matrix)
    return matrix


def solution(mesh):
    return jax.shard_map(
        body,
        mesh=mesh,
        in_specs=(P("col", "row", None, None), P(), P(), P()),
        out_specs=P("col", "row", None, None),
        check_vma=False,
    )
```

time: 763 us -> 640 us (0.84)
  waiting for transfers between devices: 657 us -> 538 us
    all_gather x2 -> x0, waiting for transfers between devices: 111 us -> none  [body(): gathered = lax.all_gather(raw_column, 'row', axis=0, tiled=True)]
    psum x2 -> x3, waiting for transfers between devices: 546 us -> 537 us  [the longest x1 247 us: body(): leading = lax.psum(leading, ('col', 'row'))]
  transfers between devices with their start and end apart: 4 -> 3, of which waited for: 4 -> 3; matrix products, arithmetic and copies ran while one was open for 1% -> 9% of each run, Pallas kernels for 0% -> 0%
where the time goes in v1:
time: 640 us; the launch traced here: 635 us
  waiting for transfers between devices  538 us (84%)
  other arithmetic  50.2 us (8%)
  between operations  25 us (4%)
  local copies, waits for them, and re-layouts  14.1 us (2%)
  matrix products  8.01 us (1%)
    psum x1, waiting for transfers between devices, body(): leading = lax.psum(leading, ('col', 'row'))  247 us
    psum x1, waiting for transfers between devices, body(): columns = lax.psum(columns, 'col')  223 us
    psum x1, waiting for transfers between devices, body(): across = lax.psum(across, 'row')  68 us
    another operation x6, other arithmetic, diag_factor(): lower_tri = jnp.linalg.cholesky(diag_tile)  24.9 us
    another operation x4, other arithmetic, diag_factor(): lax.linalg.triangular_solve(lower_tri, identity, left_side=True, lower=True)  21.2 us
  transfers between devices with their start and end apart: 3, of which 3 were waited for; matrix products, arithmetic and copies ran while one was open for 9% of the time, Pallas kernels for 0%

profile of v1, /device:TPU:1, one launch (start us, length us, event | category | flops | bytes accessed | tf_op | source)
XLA Modules:
  0.0 634.9 jit_solution(721035096207208400)
XLA Ops:
  6.5 0.7 copy-done.8
  7.2 0.7 fusion.39
  13.3 0.7 fusion.38
  19.4 1.6 copy.39
  21.1 0.7 pad_maximum_fusion.1
  21.8 0.2 fusion.30
  22.0 0.2 select_reduce_fusion.1
  22.3 0.6 slice.73
  23.0 0.6 gather_fusion.4
  23.6 0.1 copy.46
  23.7 0.9 dynamic-slice_select_fusion.1
  24.6 0.6 gather_fusion.3
  25.2 0.6 gather_fusion.1
  25.8 0.6 gather_fusion.2
  26.4 0.6 gather_fusion
  27.1 0.2 slice_reduce_fusion.1
  27.3 0.2 slice_reduce_fusion.2
  28.1 1.1 pad_maximum_fusion
  29.2 246.6 %all-reduce.4.cloned.1.call-done = f32[3,128,128]{1,2,0:T(8,128)} async-done(((f32[3,128,128]{1,2,0:T(8,128)}), f32[3,128,128]{1,2,0:T(8,128)}) %all-reduce.4.cloned.1.call-update) | async-done | bytes 196624 | tf_op jit(solution)/shard_map/psum | solution.py:46
  275.9 0.9 copy-done.6
  276.9 11.7 %cholesky.44 = f32[128,128]{1,0:T(8,128)S(1)} custom-call(f32[128,128]{1,0:T(8,128)S(1)} %fusion.15), custom_call_target="Cholesky" | custom-call | tf_op jit(solution)/shard_map/jit(cholesky)/cholesky | solution.py:17
  288.6 0.7 compare_reduce_fusion.1
  289.3 0.7 fusion.28
  290.1 9.8 %custom-call.6 = f32[1,128,128]{1,2,0:T(8,128)S(1)} custom-call(f32[1,128,128]{2,1,0:T(8,128)S(1)} %get-tuple-element.17), custom_call_target="InvertDiagBlocksLowerTriangular" | custom-call | tf_op jit(solution)/shard_map/triangular_solve/custom-call.0 | solution.py:19
  299.9 0.3 fusion.13
  300.2 0.3 convolution_multiply_fusion
  300.5 0.3 convolution_subtract_fusion
  300.7 0.1 copy.44
  300.8 11.7 %cholesky.55 = f32[128,128]{1,0:T(8,128)S(1)} custom-call(f32[128,128]{1,0:T(8,128)S(1)} %fusion.21), custom_call_target="Cholesky" | custom-call | tf_op jit(solution)/shard_map/jit(cholesky)/cholesky | solution.py:17
  312.6 0.7 compare_reduce_fusion
  313.3 0.7 select_bitcast_fusion.1
  314.0 10.0 %custom-call.7 = f32[1,128,128]{1,2,0:T(8,128)S(1)} custom-call(f32[1,128,128]{2,1,0:T(8,128)S(1)} %get-tuple-element.15), custom_call_target="InvertDiagBlocksLowerTriangular" | custom-call | tf_op jit(solution)/shard_map/triangular_solve/custom-call.0 | solution.py:19
  324.1 0.1 copy.50
  324.2 0.3 convolution_bitcast_fusion
  324.5 223.0 %all-reduce.6.cloned.1.call-done = f32[2,8,128,128]{3,2,1,0:T(8,128)} async-done(((f32[2,8,128,128]{3,2,1,0:T(8,128)}), f32[2,8,128,128]{3,2,1,0:T(8,128)}) %all-reduce.6.cloned.1.call-update) | async-done | bytes 1048592 | tf_op jit(solution)/shard_map/psum | solution.py:55
  547.4 1.9 gather_fusion.5
  549.3 0.8 select_bitcast_fusion
  550.2 0.6 convolution_select_fusion.3
  550.8 1.6 fusion.6
  552.4 1.0 copy.51
  553.4 0.6 convolution_select_fusion.1
  554.0 1.0 copy.49
  555.0 68.0 %all-reduce.8.cloned.1.call-done = f32[2,2,128,128]{3,2,0,1:T(8,128)} async-done(((f32[2,2,128,128]{3,2,0,1:T(8,128)}), f32[2,2,128,128]{3,2,0,1:T(8,128)}) %all-reduce.8.cloned.1.call-update) | async-done | bytes 262160 | tf_op jit(solution)/shard_map/psum | solution.py:59
  622.9 1.3 convolution_select_fusion.6
  624.2 1.2 fusion.7
  625.4 0.3 convolution_select_fusion.4
  625.7 1.4 fusion.5
  627.1 1.3 copy.56
  (48 shorter events, 0.7 us)
Async XLA Ops:
  6.5 0.7 copy-start.8
  6.5 269.3 %all-reduce.4.cloned.1.call-start = ((), (), s32[]{:S(2)}) async-start(), calls=%async_computation | async-start | bytes 393216 | tf_op jit(solution)/shard_map/psum | solution.py:46
  12.6 0.7 copy-start
  19.4 2.9 copy-start.7
  21.0 2.8 copy-start.1
  21.8 525.7 %all-reduce.6.cloned.1.call-start = ((), (), s32[]{:S(2)}) async-start(), calls=%async_computation.1 | async-start | bytes 2097152 | tf_op jit(solution)/shard_map/psum | solution.py:55
  25.7 2.4 copy-start.4
  275.8 0.9 copy-start.6
  275.9 347.1 %all-reduce.8.cloned.1.call-start = ((), (), s32[]{:S(2)}) async-start(), calls=%async_computation.2 | async-start | bytes 524288 | tf_op jit(solution)/shard_map/psum | solution.py:59
  547.4 2.7 copy-start.5
  622.9 2.8 copy-start.2
  622.9 2.8 copy-start.3
Sparse Core Ops, SparseCore 0:
  21.9 253.8 all-reduce.3
  278.4 268.9 all-reduce.5
  550.3 72.5 all-reduce.7
